TPU v7x, 32 devices: a whole 2x2x4 slice. The times are simulated.
32 devices in a mesh: grp: 4 (over y, x), tp: 8 (over z, core).
Axes of the slice: x: 2, y: 2, z: 4, core: 2. Of those that a mesh axis runs over, the one named last changes fastest.
Arguments:
- layer_input: bfloat16 [8192, 2048], P('grp'), may hold values from -6 to 6
- out_cotangent: bfloat16 [8192, 2048], P('grp'), may hold values from -6 to 6
- seq_group: int32 [6], replicated, may hold values from 0 to 3, as said below
- seq_len: int32 [6], replicated, may hold values from 512 to 2048, as said below
- w_qkv: float32 [2048, 6144], P('grp', 'tp'), may hold values from -0.1875 to 0.1875
- b_qv: float32 [4096], replicated, may hold values from -3 to 3
- w_out: float32 [2048, 2048], P('grp', 'tp'), may hold values from -0.75 to 0.75
- b_out: float32 [2048], replicated, may hold values from -2 to 2
- w_up: float32 [2048, 8192], P('grp', 'tp'), may hold values from -0.125 to 0.125
- b_up: float32 [8192], replicated, may hold values from -3 to 3
- w_down: float32 [2048, 8192], P('grp', 'tp'), may hold values from -0.0625 to 0.0625
- b_down: float32 [2048], replicated, may hold values from -2 to 2
- first_norm_gain: float32 [2048], replicated, may hold values from 0.1 to 1.9
- first_norm_bias: float32 [2048], replicated, may hold values from -2 to 2
- second_norm_gain: float32 [2048], replicated, may hold values from 0.1 to 1.9
- second_norm_bias: float32 [2048], replicated, may hold values from -2 to 2
Outputs:
- layer_output: bfloat16 [8192, 2048], P(('grp', 'tp'))
- grad_x: float32 [8192, 2048], P(('grp', 'tp'))
- grad_w_qkv: float32 [2048, 6144], P('grp', 'tp')
- grad_b_qv: float32 [4096], replicated
- grad_w_out: float32 [2048, 2048], P('grp', 'tp')
- grad_b_out: float32 [2048], replicated
- grad_w_up: float32 [2048, 8192], P('grp', 'tp')
- grad_b_up: float32 [8192], replicated
- grad_w_down: float32 [2048, 8192], P('grp', 'tp')
- grad_b_down: float32 [2048], replicated
- grad_ln1_gain: float32 [2048], replicated
- grad_ln1_bias: float32 [2048], replicated
- grad_ln2_gain: float32 [2048], replicated
- grad_ln2_bias: float32 [2048], replicated
Inputs may be any that keep to these rules, and one draw needn't show every extreme that they name: `seq_group`: each group's sequences total at most 2048 tokens, and in every draw some group holds exactly 2048; every group holds at least one sequence. `seq_len`: each sequence has 2048 or 512 tokens.
All inputs are finite; a program needn't handle non-finite values.
Results may differ from a plain program's by a relative error of at most 0.023.
Values may be sent and summed in bfloat16 or wider, within the bound.
A program may use at most 320 MiB of HBM per device.

v0:
```python
import jax
import jax.numpy as jnp
from jax import lax
from jax.sharding import PartitionSpec as P

HD = 128


def layer_normalize(rows, gain, bias):
    mean_row = jnp.mean(rows, -1, keepdims=True)
    centred = rows - mean_row
    inverse = lax.rsqrt(jnp.mean(centred * centred, -1, keepdims=True) + 1e-05)
    normed = centred * inverse
    return (normed * gain + bias, normed, inverse)


def norm_backward_pass(grad_norm, normed, inverse, gain):
    scaled = grad_norm * gain
    inner = jnp.mean(scaled, -1, keepdims=True) + normed * jnp.mean(
        scaled * normed, -1, keepdims=True
    )
    return inverse * (scaled - inner)


def contract(left, right, left_dim, right_dim):
    return lax.dot_general(
        left, right, (((left_dim,), (right_dim,)), ((), ())), preferred_element_type=jnp.float32
    )


def activate(values_in):
    return jax.nn.gelu(values_in, approximate=True)


def on_device(
    layer_input,
    out_cotangent,
    seq_group,
    seq_len,
    w_qkv,
    b_qv,
    w_out,
    b_out,
    w_up,
    b_up,
    w_down,
    b_down,
    first_norm_gain,
    first_norm_bias,
    second_norm_gain,
    second_norm_bias,
):
    w_attn, w_proj, w_expand, w_reduce = (
        lax.all_gather(w_qkv.astype(jnp.bfloat16), "grp", axis=0, tiled=True),
        lax.all_gather(w_out.astype(jnp.bfloat16), "grp", axis=0, tiled=True),
        lax.all_gather(w_up.astype(jnp.bfloat16), "grp", axis=0, tiled=True),
        lax.all_gather(w_down.astype(jnp.bfloat16), "grp", axis=0, tiled=True),
    )
    tp_rank = lax.axis_index("tp")
    tp_count = lax.axis_size("tp")
    group_rank = lax.axis_index("grp")
    length = layer_input.shape[0]
    shared_row_block = length // tp_count
    local_row_start = tp_rank * shared_row_block
    heads_here = w_proj.shape[1] // HD
    hidden_here = w_expand.shape[1]
    seq_count = seq_group.shape[0]
    in_group = seq_group == group_rank
    lengths = jnp.where(in_group, seq_len, 0)
    seq_order = jnp.arange(seq_count, dtype=jnp.int32)
    earlier = seq_order[:, None] > seq_order[None, :]
    offsets = jnp.sum(jnp.where(earlier, lengths[None, :], 0), 1)
    places = jnp.arange(length, dtype=jnp.int32)
    inside = (
        in_group[None, :]
        & (places[:, None] >= offsets[None, :])
        & (places[:, None] < (offsets + lengths)[None, :])
    )
    segment = jnp.sum(jnp.where(inside, seq_order[None, :] + 1, 0), 1) - 1
    live_rows = (segment >= 0).astype(jnp.float32)[:, None]
    input_row_block = layer_input.astype(jnp.float32)
    first_normalized, first_standardized, first_inverse_deviation = layer_normalize(
        input_row_block, first_norm_gain, first_norm_bias
    )
    normed_oneb = first_normalized.astype(jnp.bfloat16)
    head_bias = lax.dynamic_slice_in_dim(
        b_qv.reshape(-1, 2, HD), tp_rank * heads_here, heads_here, 0
    )
    bias_three = jnp.stack(
        [head_bias[:, 0], jnp.zeros_like(head_bias[:, 0]), head_bias[:, 1]], 1
    ).reshape(-1)
    projected = (
        jnp.dot(normed_oneb, w_attn, preferred_element_type=jnp.float32) + bias_three
    ).astype(jnp.bfloat16)
    projected = projected.reshape(length, heads_here, 3, HD)
    query = projected[:, :, 0]
    keys = projected[:, :, 1]
    values = projected[:, :, 2]
    block_rows = min(512, length)
    blocks = length // block_rows
    score_scale = HD ** (-0.5)
    columns = jnp.arange(length, dtype=jnp.int32)

    def scores_for(block_index):
        first_row = block_index * block_rows
        query_block = lax.dynamic_slice_in_dim(query, first_row, block_rows, 0)
        dotted = (
            jnp.einsum("qhe,khe->hqk", query_block, keys, preferred_element_type=jnp.float32)
            * score_scale
        )
        segment_block = lax.dynamic_slice_in_dim(segment, first_row, block_rows, 0)
        row_places = first_row + jnp.arange(block_rows, dtype=jnp.int32)
        allowed = (segment_block[:, None] == segment[None, :]) & (
            columns[None, :] <= row_places[:, None]
        )
        return (jnp.where(allowed[None], dotted, -1e30), query_block)

    def attend(block_index):
        masked, unused = scores_for(block_index)
        highest_score = jnp.max(masked, -1, keepdims=True)
        powers = jnp.exp(masked - highest_score)
        summed = jnp.sum(powers, -1, keepdims=True)
        chances = (powers / summed).astype(jnp.bfloat16)
        context = jnp.einsum(
            "hqk,khe->qhe", chances, values, preferred_element_type=jnp.float32
        ).astype(jnp.bfloat16)
        return (context, highest_score[..., 0] + jnp.log(summed[..., 0]))

    contexts, log_totals = lax.map(attend, jnp.arange(blocks))
    context_all = contexts.reshape(length, heads_here * HD)
    attn_total = lax.psum(contract(context_all, w_proj, 1, 1).astype(jnp.bfloat16), "tp").astype(
        jnp.float32
    )
    hidden_input = input_row_block + attn_total + b_out
    second_normalized, second_standardized, second_inverse_deviation = layer_normalize(
        hidden_input, second_norm_gain, second_norm_bias
    )
    normed_twob = second_normalized.astype(jnp.bfloat16)
    up_bias = lax.dynamic_slice_in_dim(b_up, tp_rank * hidden_here, hidden_here, 0)
    before = jnp.dot(normed_twob, w_expand, preferred_element_type=jnp.float32) + up_bias
    active = activate(before).astype(jnp.bfloat16)
    live_share = lax.dynamic_slice_in_dim(live_rows, local_row_start, shared_row_block, 0)
    mlp_total = lax.psum(contract(active, w_reduce, 1, 1).astype(jnp.bfloat16), "tp").astype(
        jnp.float32
    )
    out_share = (
        lax.dynamic_slice_in_dim(hidden_input, local_row_start, shared_row_block, 0)
        + lax.dynamic_slice_in_dim(mlp_total, local_row_start, shared_row_block, 0)
        + b_down
    )
    result = (live_share * out_share).astype(jnp.bfloat16)
    output_gradient = out_cotangent.astype(jnp.float32) * live_rows
    grad_outb = output_gradient.astype(jnp.bfloat16)
    grad_share = lax.dynamic_slice_in_dim(output_gradient, local_row_start, shared_row_block, 0)
    grad_reduce = contract(grad_outb, active, 0, 0)
    grad_active = jnp.dot(grad_outb, w_reduce, preferred_element_type=jnp.float32)
    unused, gelu_back = jax.vjp(activate, before)
    grad_beforeb = gelu_back(grad_active)[0].astype(jnp.bfloat16)
    grad_expand = contract(normed_twob, grad_beforeb, 0, 0)
    up_bias_part = jnp.sum(grad_beforeb.astype(jnp.float32), 0)
    second_norm_gradient = lax.psum(
        contract(grad_beforeb, w_expand, 1, 1).astype(jnp.bfloat16), "tp"
    ).astype(jnp.float32)
    hidden_gradient = output_gradient + norm_backward_pass(
        second_norm_gradient, second_standardized, second_inverse_deviation, second_norm_gain
    )
    grad_resb = hidden_gradient.astype(jnp.bfloat16)
    residual_share_gradient = lax.dynamic_slice_in_dim(
        hidden_gradient, local_row_start, shared_row_block, 0
    )
    second_norm_shared = lax.dynamic_slice_in_dim(
        second_norm_gradient, local_row_start, shared_row_block, 0
    )
    gain_two_grad = jnp.sum(
        second_norm_shared
        * lax.dynamic_slice_in_dim(second_standardized, local_row_start, shared_row_block, 0),
        0,
    )
    bias_two_grad = jnp.sum(second_norm_shared, 0)
    bias_out_grad = jnp.sum(residual_share_gradient, 0)
    down_bias_grad = jnp.sum(grad_share, 0)
    grad_proj = contract(grad_resb, context_all, 0, 0)
    grad_context = (
        jnp.dot(grad_resb, w_proj, preferred_element_type=jnp.float32)
        .astype(jnp.bfloat16)
        .reshape(length, heads_here, HD)
    )

    def attend_back(running, block_index):
        grad_keys, grad_values = running
        masked, query_block = scores_for(block_index)
        chances = jnp.exp(masked - log_totals[block_index][..., None])
        grad_block = lax.dynamic_slice_in_dim(grad_context, block_index * block_rows, block_rows, 0)
        grad_values = grad_values + jnp.einsum(
            "hqk,qhe->khe",
            chances.astype(jnp.bfloat16),
            grad_block,
            preferred_element_type=jnp.float32,
        )
        grad_chances = jnp.einsum(
            "qhe,khe->hqk", grad_block, values, preferred_element_type=jnp.float32
        )
        grad_scores = (
            chances * (grad_chances - jnp.sum(chances * grad_chances, -1, keepdims=True))
        ).astype(jnp.bfloat16)
        grad_query = (
            jnp.einsum("hqk,khe->qhe", grad_scores, keys, preferred_element_type=jnp.float32)
            * score_scale
        )
        grad_keys = (
            grad_keys
            + jnp.einsum(
                "hqk,qhe->khe", grad_scores, query_block, preferred_element_type=jnp.float32
            )
            * score_scale
        )
        return ((grad_keys, grad_values), grad_query)

    zeros_heads = jnp.zeros((length, heads_here, HD), jnp.float32)
    (grad_keys, grad_values), grad_queries = lax.scan(
        attend_back, (zeros_heads, zeros_heads), jnp.arange(blocks)
    )
    grad_queries = grad_queries.reshape(length, heads_here, HD)
    grad_projected = (
        jnp.stack([grad_queries, grad_keys, grad_values], 2)
        .astype(jnp.bfloat16)
        .reshape(length, heads_here * 3 * HD)
    )
    grad_attn = contract(normed_oneb, grad_projected, 0, 0)
    projected_sums = jnp.sum(grad_projected.astype(jnp.float32), 0).reshape(heads_here, 3, HD)
    query_value = jnp.stack([projected_sums[:, 0], projected_sums[:, 2]], 1)
    query_value_full = lax.dynamic_update_slice_in_dim(
        jnp.zeros((b_qv.shape[0] // (2 * HD), 2, HD), jnp.float32),
        query_value,
        tp_rank * heads_here,
        0,
    ).reshape(-1)
    up_bias_full = lax.dynamic_update_slice_in_dim(
        jnp.zeros(b_up.shape, jnp.float32), up_bias_part, tp_rank * hidden_here, 0
    )
    first_norm_gradient = lax.dynamic_slice_in_dim(
        lax.psum(contract(grad_projected, w_attn, 1, 1).astype(jnp.bfloat16), "tp").astype(
            jnp.float32
        ),
        local_row_start,
        shared_row_block,
        0,
    )
    shared_standardized = lax.dynamic_slice_in_dim(
        first_standardized, local_row_start, shared_row_block, 0
    )
    shared_inverse_deviation = lax.dynamic_slice_in_dim(
        first_inverse_deviation, local_row_start, shared_row_block, 0
    )
    input_gradient = residual_share_gradient + norm_backward_pass(
        first_norm_gradient, shared_standardized, shared_inverse_deviation, first_norm_gain
    )
    first_gain_gradient = jnp.sum(first_norm_gradient * shared_standardized, 0)
    bias_one_grad = jnp.sum(first_norm_gradient, 0)
    grads_attn, grads_proj, grads_expand, grads_reduce = (
        lax.psum_scatter(
            grad_attn.astype(jnp.bfloat16), "grp", scatter_dimension=0, tiled=True
        ).astype(jnp.float32),
        lax.psum_scatter(
            grad_proj.astype(jnp.bfloat16), "grp", scatter_dimension=0, tiled=True
        ).astype(jnp.float32),
        lax.psum_scatter(
            grad_expand.astype(jnp.bfloat16), "grp", scatter_dimension=0, tiled=True
        ).astype(jnp.float32),
        lax.psum_scatter(
            grad_reduce.astype(jnp.bfloat16), "grp", scatter_dimension=0, tiled=True
        ).astype(jnp.float32),
    )
    small_grads = lax.psum(
        (
            query_value_full,
            bias_out_grad,
            up_bias_full,
            down_bias_grad,
            first_gain_gradient,
            bias_one_grad,
            gain_two_grad,
            bias_two_grad,
        ),
        ("grp", "tp"),
    )
    return (
        result,
        input_gradient,
        grads_attn,
        small_grads[0],
        grads_proj,
        small_grads[1],
        grads_expand,
        small_grads[2],
        grads_reduce,
        small_grads[3],
        small_grads[4],
        small_grads[5],
        small_grads[6],
        small_grads[7],
    )


def solution(mesh):
    in_specs = (
        P("grp", None),
        P("grp", None),
        P(),
        P(),
        P("grp", "tp"),
        P(),
        P("grp", "tp"),
        P(),
        P("grp", "tp"),
        P(),
        P("grp", "tp"),
        P(),
        P(),
        P(),
        P(),
        P(),
    )
    out_specs = (
        P(("grp", "tp"), None),
        P(("grp", "tp"), None),
        P("grp", "tp"),
        P(),
        P("grp", "tp"),
        P(),
        P("grp", "tp"),
        P(),
        P("grp", "tp"),
        P(),
        P(),
        P(),
        P(),
        P(),
    )
    return jax.shard_map(
        on_device, mesh=mesh, in_specs=in_specs, out_specs=out_specs, check_vma=False
    )
```

profile of v0, /device:TPU:8, one launch (start us, length us, event | category | flops | bytes accessed | tf_op | source)
XLA Modules:
  0.0 1345.7 jit_solution(15598600205464487332)
XLA Ops:
  21.6 34.0 %all-gather.5.cloned.1.call-done = bf16[2048,768]{1,0:T(8,128)(2,1)} async-done(((bf16[512,768]{1,0:T(8,128)(2,1)}), bf16[2048,768]{1,0:T(8,128)(2,1)}) %all-gather.5.cloned.1.call-update) | async-done | bytes 3145744 | tf_op jit(solution)/shard_map/all_gather | solution.py:54
  55.6 11.5 add_convert_fusion.2
  71.4 46.1 %while.28 = (s32[]{:T(128)}, bf16[4,512,2,128]{3,2,1,0:T(2,128)(2,1)}, f32[4,2,512]{2,1,0:T(2,128)}, s32[4]{0:T(128)S(1)}, s32[2048]{0:T(1024)S(1)}, /*index=5*/...) while((s32[]{:T(128)}, ...), condition=%wide.region_7.8_spmd.clone, body=%wide.region_4.7_spmd.clone.sunk | while | flops 1102183936 | bytes 32557260 | solution.py:129
  132.2 169.3 %all-reduce.7.cloned.1.call-done = bf16[2048,2048]{1,0:T(8,128)(2,1)} async-done(((bf16[2048,2048]{1,0:T(8,128)(2,1)}), bf16[2048,2048]{1,0:T(8,128)(2,1)}) %all-reduce.7.cloned.1.call-update) | async-done | bytes 8388624 | tf_op jit(solution)/shard_map/psum | solution.py:131
  301.5 17.6 %fusion.88 = (f32[2048]{0:T(1024)S(1)}, f32[2048,2048]{1,0:T(8,128)}, f32[2048,2048]{1,0:T(8,128)}) fusion(f32[2048]{0:T(1024)S(1)} %copy-done.25, bf16[2048,2048]{1,0:T(8,128)(2,1)} %all-reduce.7.cloned.1.call-done, bf16[2048,2048]{1,0:T(8,128)(2,1)} %param.20, f32[2048]{0:T(1024)S(1)} %add_rsqrt_fusion.1, f32[2048]{0:T(1024)S(1)} %broadcast_multiply_fusion.3), kind=kLoop, calls=%fused_computation.141 | loop fusion | flops 29358080 | bytes 50364416 | tf_op jit(solution)/shard_map/reduce_sum | solution.py:10
  326.7 11.8 subtract_multiply_fusion
  338.5 18.2 %all-gather.9.cloned.1.call-done = bf16[2048,1024]{1,0:T(8,128)(2,1)} async-done(((bf16[512,1024]{1,0:T(8,128)(2,1)}), bf16[2048,1024]{1,0:T(8,128)(2,1)}) %all-gather.9.cloned.1.call-update) | async-done | bytes 4194320 | tf_op jit(solution)/shard_map/all_gather | solution.py:56
  356.7 15.5 %fusion.75 = f32[2048,1024]{1,0:T(8,128)} fusion(bf16[2048,1024]{1,0:T(8,128)(2,1)} %all-gather.9.cloned.1.call-done, f32[2048,2048]{1,0:T(8,128)} %subtract_multiply_fusion, f32[2048]{0:T(1024)S(1)} %copy-done.31, f32[2048]{0:T(1024)S(1)} %copy-done.21), kind=kOutput, calls=%fused_computation.102 | convolution fusion | flops 8602517504 | bytes 29376512 | tf_op jit(solution)/shard_map/dot_general | solution.py:140
  372.2 39.5 %all-gather.11.cloned.1.call-done = bf16[2048,1024]{1,0:T(8,128)(2,1)} async-done(((bf16[512,1024]{1,0:T(8,128)(2,1)}), bf16[2048,1024]{1,0:T(8,128)(2,1)}) %all-gather.11.cloned.1.call-update) | async-done | bytes 4194320 | tf_op jit(solution)/shard_map/all_gather | solution.py:57
  411.7 19.5 %convert_reduce_fusion.1 = (f32[1024]{0:T(1024)}, bf16[2048,1024]{1,0:T(8,128)(2,1)S(1)}) fusion(f32[2048,1024]{1,0:T(8,128)} %fusion.75, f32[1024]{0:T(1024)S(1)} %dynamic_slice.59, bf16[2048,1024]{1,0:T(8,128)(2,1)} %all-gather.11.cloned.1.call-done, f32[2048]{0:T(1024)S(1)} %compare_convert_fusion, bf16[2048,2048]{1,0:T(8,128)(2,1)} %param.21), kind=kOutput, calls=%fused_computation.74 | convolution fusion | flops 8650750976 | bytes 25182208 | tf_op jit(solution)/shard_map/dot_general | solution.py:156
  433.2 10.9 convolution_convert_fusion.1
  444.1 175.7 %all-reduce.9.cloned.1.call-done = bf16[2048,2048]{1,0:T(8,128)(2,1)} async-done(((bf16[2048,2048]{1,0:T(8,128)(2,1)}), bf16[2048,2048]{1,0:T(8,128)(2,1)}) %all-reduce.9.cloned.1.call-update) | async-done | bytes 8388624 | tf_op jit(solution)/shard_map/psum | solution.py:161
  619.8 10.5 multiply_reduce_fusion.3
  630.3 19.1 %convert_multiply_fusion = (f32[2048,2048]{1,0:T(8,128)}, f32[2048,2048]{1,0:T(8,128)S(1)}) fusion(bf16[2048,2048]{1,0:T(8,128)(2,1)} %param.21, f32[2048]{0:T(1024)S(1)} %compare_convert_fusion, f32[2048]{0:T(1024)S(1)} %broadcast_multiply_fusion, f32[2048]{0:T(1024)S(1)} %broadcast_multiply_fusion.1, f32[2048]{0:T(1024)S(1)} %copy-done.21, ...), kind=kLoop, calls=%fused_computation.59 | loop fusion | flops 46137344 | bytes 67158016 | tf_op jit(solution)/shard_map/mul | solution.py:152
  658.8 16.8 %fusion.61 = bf16[2048,1024]{1,0:T(8,128)(2,1)} fusion(bf16[2048,2048]{1,0:T(8,128)(2,1)} %param.21, f32[2048]{0:T(1024)S(1)} %compare_convert_fusion, f32[2048,1024]{1,0:T(8,128)} %fusion.75, f32[1024]{0:T(1024)S(1)} %dynamic_slice.59), kind=kOutput, calls=%fused_computation.91 | convolution fusion | flops 8625586176 | bytes 20983808 | tf_op jit(solution)/shard_map/dot_general | solution.py:26
  675.7 15.3 %convolution_convert_fusion.4 = bf16[2048,1024]{1,0:T(8,128)(2,1)} fusion(bf16[2048,1024]{1,0:T(8,128)(2,1)} %copy-done.34, f32[2048,2048]{1,0:T(8,128)} %subtract_multiply_fusion, f32[2048]{0:T(1024)S(1)} %copy-done.31, f32[2048]{0:T(1024)S(1)} %copy-done.21), kind=kOutput, calls=%fused_computation.92 | convolution fusion | flops 8604614656 | bytes 25182208 | tf_op jit(solution)/shard_map/dot_general | solution.py:26
  691.1 9.8 fusion.67
  700.9 89.8 %while.29 = (s32[]{:T(128)}, f32[2048,2,128]{0,2,1:T(8,128)S(1)}, f32[2048,2,128]{0,2,1:T(8,128)}, bf16[4,512,2,128]{3,1,0,2:T(8,128)(2,1)}, s32[4]{0:T(128)S(1)...) while((s32[]{:T(128)}, f32[2048,2,128]{0,2,1:T(8,128)S(1)}, ...), condition=%wide.region_17.18_spmd.clone, body=%wide.region_15.17_spmd.clone.sunk | while | flops 2721709568 | bytes 97040784 | solution.py:220
  800.1 13.1 convolution_convert_fusion.5
  813.2 17.8 %convolution_convert_fusion.2 = bf16[2048,2048]{1,0:T(8,128)(2,1)} fusion(bf16[2048,1024]{1,0:T(8,128)(2,1)} %all-gather.11.cloned.1.call-done, f32[2048,1024]{1,0:T(8,128)} %fusion.75, f32[1024]{0:T(1024)S(1)} %copy-done.28), kind=kOutput, calls=%fused_computation.78 | convolution fusion | flops 8615100416 | bytes 20975616 | tf_op jit(solution)/shard_map/dot_general | solution.py:26
  831.1 9.2 convolution_convert_fusion
  841.7 11.3 convert_element_type.149
  868.6 325.1 %all-reduce.13.cloned.1.call-done = (bf16[2048,2048]{1,0:T(8,128)(2,1)}, bf16[2048,2048]{1,0:T(8,128)(2,1)}) async-done(((bf16[2048,2048]{1,0:T(8,128)(2,1)}, bf16[2048,2048]{1,0:T(8,128)(2,1)}), (bf16[2048,2048]{1,0:T(8,128)(2,1)}, bf16[2048,2048]{1,0:T(8,128)(2,1)})) %all-reduce.13.cloned.1.call-update) | async-done | bytes 16777232 | tf_op jit(solution)/shard_map/psum | solution.py:143
  1205.3 122.7 %all-reduce.11.cloned.1.call-done = (f32[4096]{0:T(1024)}, f32[2048]{0:T(1024)}, f32[8192]{0:T(1024)}, f32[2048]{0:T(1024)}, f32[2048]{0:T(1024)}, /*index=5*/f32[2048]{0:T(1024)}, f32[2048]{0:T(1024)}, f32[2048]{0:T(1024)}) async-done(((f32[4096]{0:T(1024)}, f32[2048]{0:T(1024)}, f32[8192]{0:T(1024)}, f32[2048]{0:T(1024)}, f32[2048]{0:T(1024)}, /*index=5*/f32[2048]{0:T(1024)}, f32[2048]{0:T(1024)}, ...) | async-done | bytes 98320 | tf_op jit(solution)/shard_map/psum | solution.py:274
  (271 shorter events, 222.6 us)
Async XLA Ops:
  7.2 48.4 %all-gather.5.cloned.1.call-start = ((), (), s32[]{:S(2)}) async-start(), calls=%async_computation.4 | async-start | bytes 3932160 | tf_op jit(solution)/shard_map/all_gather | solution.py:54
  9.6 107.9 %all-gather.7.cloned.1.call-start = ((), (), s32[]{:S(2)}) async-start(), calls=%async_computation.5 | async-start | bytes 1310720 | tf_op jit(solution)/shard_map/all_gather | solution.py:55
  11.5 290.1 %all-reduce.7.cloned.1.call-start = ((), (), s32[]{:S(2)}) async-start(), calls=%async_computation.6 | async-start | bytes 16777216 | tf_op jit(solution)/shard_map/psum | solution.py:131
  13.4 42.2 %copy-start.22 = (f32[2048]{0:T(1024)S(1)}, f32[2048]{0:T(1024)}, u32[]{:S(2)}) copy-start(f32[2048]{0:T(1024)} %param.32) | copy-start | bytes 24580
  13.4 42.2 %copy-start.32 = (f32[2048]{0:T(1024)S(1)}, f32[2048]{0:T(1024)}, u32[]{:S(2)}) copy-start(f32[2048]{0:T(1024)} %param.33) | copy-start | bytes 24580
  19.2 282.3 %copy-start.15 = (f32[2048]{0:T(1024)}, f32[2048]{0:T(1024)S(1)}, u32[]{:S(2)}) copy-start(f32[2048]{0:T(1024)S(1)} %broadcast_multiply_fusion.3) | copy-start | bytes 24580
  21.6 280.0 %copy-start.19 = (f32[2048]{0:T(1024)}, f32[2048]{0:T(1024)S(1)}, u32[]{:S(2)}) copy-start(f32[2048]{0:T(1024)S(1)} %add_rsqrt_fusion.1) | copy-start | bytes 24580
  125.8 175.8 %copy-start.25 = (f32[2048]{0:T(1024)S(1)}, f32[2048]{0:T(1024)}, u32[]{:S(2)}) copy-start(f32[2048]{0:T(1024)} %param.27) | copy-start | bytes 24580
  125.8 230.8 %all-gather.9.cloned.1.call-start = ((), (), s32[]{:S(2)}) async-start(), calls=%async_computation.7 | async-start | bytes 5242880 | tf_op jit(solution)/shard_map/all_gather | solution.py:56
  128.6 283.0 %all-gather.11.cloned.1.call-start = ((), (), s32[]{:S(2)}) async-start(), calls=%async_computation.8 | async-start | bytes 5242880 | tf_op jit(solution)/shard_map/all_gather | solution.py:57
  131.4 488.4 %all-reduce.9.cloned.1.call-start = ((), (), s32[]{:S(2)}) async-start(), calls=%async_computation.9 | async-start | bytes 16777216 | tf_op jit(solution)/shard_map/psum | solution.py:161
  131.5 527.3 %copy-start.18 = (f32[2048]{0:T(1024)}, f32[2048]{0:T(1024)S(1)}, u32[]{:S(2)}) copy-start(f32[2048]{0:T(1024)S(1)} %compare_convert_fusion) | copy-start | bytes 24580
  132.2 526.6 %copy-start.27 = (f32[1024]{0:T(1024)}, f32[1024]{0:T(1024)S(1)}, u32[]{:S(2)}) copy-start(f32[1024]{0:T(1024)S(1)} %dynamic_slice.59) | copy-start | bytes 12292
  326.7 30.0 %copy-start.21 = (f32[2048]{0:T(1024)S(1)}, f32[2048]{0:T(1024)}, u32[]{:S(2)}) copy-start(f32[2048]{0:T(1024)} %param.34) | copy-start | bytes 24580
  326.7 30.0 %copy-start.31 = (f32[2048]{0:T(1024)S(1)}, f32[2048]{0:T(1024)}, u32[]{:S(2)}) copy-start(f32[2048]{0:T(1024)} %param.35) | copy-start | bytes 24580
  444.1 414.6 %reduce-scatter.7.cloned.1.call-start = ((), (), s32[]{:S(2)}) async-start(), calls=%async_computation.11 | async-start | bytes 1310720 | tf_op jit(solution)/shard_map/reduce_scatter | solution.py:264
  630.3 24.8 %copy-start.8 = (bf16[4,512,2,128]{3,2,1,0:T(2,128)(2,1)S(1)}, bf16[4,512,2,128]{3,2,1,0:T(2,128)(2,1)}, u32[]{:S(2)}) copy-start(bf16[4,512,2,128]{3,2,1,0:T(2,128)(2,1)} %get-tuple-element.126) | copy-start | bytes 3145732
  658.7 201.7 %reduce-scatter.11.cloned.1.call-start = ((), (), s32[]{:S(2)}) async-start(), calls=%async_computation.13 | async-start | bytes 5242880 | tf_op jit(solution)/shard_map/reduce_scatter | solution.py:270
  675.7 187.6 %reduce-scatter.9.cloned.1.call-start = ((), (), s32[]{:S(2)}) async-start(), calls=%async_computation.12 | async-start | bytes 5242880 | tf_op jit(solution)/shard_map/reduce_scatter | solution.py:267
  691.1 174.9 %reduce-scatter.5.cloned.1.call-start = ((), (), s32[]{:S(2)}) async-start(), calls=%async_computation.10 | async-start | bytes 3932160 | tf_op jit(solution)/shard_map/reduce_scatter | solution.py:261
  813.2 380.5 %all-reduce.13.cloned.1.call-start = ((), (), s32[]{:S(2)}) async-start(), calls=%async_computation.15 | async-start | bytes 33554432 | tf_op jit(solution)/shard_map/psum | solution.py:143
  840.2 487.7 %all-reduce.11.cloned.1.call-start = ((), (), s32[]{:S(2)}) async-start(), calls=%async_computation.14 | async-start | bytes 196608 | tf_op jit(solution)/shard_map/psum | solution.py:274
  858.6 343.5 %copy-start.17 = (f32[16,2,128]{2,1,0:T(2,128)}, f32[16,2,128]{2,1,0:T(2,128)S(1)}, u32[]{:S(2)}) copy-start(f32[16,2,128]{2,1,0:T(2,128)S(1)} %constant_dynamic-update-slice_fusion) | copy-start | bytes 49156
  863.2 338.9 %copy-start.24 = (f32[2048]{0:T(1024)S(1)}, f32[2048]{0:T(1024)}, u32[]{:S(2)}) copy-start(f32[2048]{0:T(1024)} %param.31) | copy-start | bytes 24580
  (35 other events, 237.0 us)
Sparse Core Ops, SparseCore 0:
  10.4 45.1 all-gather.4
  58.0 26.6 all-gather.6
  125.9 175.5 all-reduce.6
  303.8 52.8 all-gather.8
  358.9 52.6 all-gather.10
  444.2 175.5 all-reduce.8
  658.8 27.8 reduce-scatter.6
  690.0 52.6 reduce-scatter.10
  745.7 52.6 reduce-scatter.8
  813.3 43.9 reduce-scatter.4
  860.1 333.5 all-reduce.12
  1202.2 125.6 all-reduce.10
where the time goes:
time: 1350 us
  waiting for transfers between devices  885 us (66%)
  matrix products  229 us (17%)
  other arithmetic  157 us (12%)
  local copies, waits for them, and re-layouts  45.9 us (3%)
  between operations  15.2 us (1%)
  loops' own time  14 us (1%)
    psum x1, waiting for transfers between devices, on_device(): lax.psum(contract(active, w_reduce, 1, 1).astype(jnp.bfloat16), 'tp')  325 us
    psum x1, waiting for transfers between devices, on_device(): lax.psum(contract(grad_beforeb, w_expand, 1, 1).astype(jnp.bfloat16), 'tp')  176 us
    psum x1, waiting for transfers between devices, on_device(): lax.psum(contract(context_all, w_proj, 1, 1).astype(jnp.bfloat16), 'tp')  169 us
    psum x1, waiting for transfers between devices, on_device(): lax.psum((query_value_full, bias_out_grad, up_bias_full, down_bias_grad,...  123 us
    dot_general x8, matrix products, contract(): lax.dot_general(left, right, (((left_dim,), (right_dim,)), ((), ())), pre...  94.9 us
    all_gather x1, waiting for transfers between devices, on_device(): lax.all_gather(w_down.astype(jnp.bfloat16), 'grp', axis=0, tiled=True)  39.5 us
    all_gather x1, waiting for transfers between devices, on_device(): lax.all_gather(w_qkv.astype(jnp.bfloat16), 'grp', axis=0, tiled=True)  34 us
  transfers between devices with their start and end apart: 12, of which 7 were waited for; matrix products, arithmetic and copies ran while one was open for 24% of the time, Pallas kernels for 0%

commit v1 on v0

--- a/solution.py
+++ b/solution.py
@@ -271,7 +271,7 @@
             grad_reduce.astype(jnp.bfloat16), "grp", scatter_dimension=0, tiled=True
         ).astype(jnp.float32),
     )
-    small_grads = lax.psum(
+    one_axis = lax.psum(
         (
             query_value_full,
             bias_out_grad,
@@ -282,8 +282,9 @@
             gain_two_grad,
             bias_two_grad,
         ),
-        ("grp", "tp"),
-    )
+        "tp",
+    )
+    small_grads = lax.psum(one_axis, "grp")
     return (
         result,
         input_gradient,

time: 1350 us -> 1430 us (1.059)
  waiting for transfers between devices: 885 us -> 953 us
    psum x1, waiting for transfers between devices: 123 us -> 55.9 us  [on_device(): lax.psum((query_value_full, bias_out_grad, up_bias_full, down_bias_grad,...]
    psum x1, waiting for transfers between devices: 325 us -> 260 us  [on_device(): lax.psum(contract(active, w_reduce, 1, 1).astype(jnp.bfloat16), 'tp')]
    reduce_scatter x1, waiting for transfers between devices: 0.01 us -> 54.2 us  [on_device(): lax.psum_scatter(grad_reduce.astype(jnp.bfloat16), 'grp', scatter_dimensi...]
    reduce_scatter x1, waiting for transfers between devices: 0.01 us -> 52.7 us  [on_device(): lax.psum_scatter(grad_expand.astype(jnp.bfloat16), 'grp', scatter_dimensi...]
    reduce_scatter x1, waiting for transfers between devices: 0.01 us -> 44.5 us  [on_device(): lax.psum_scatter(grad_attn.astype(jnp.bfloat16), 'grp', scatter_dimension...]
    psum x0 -> x1, waiting for transfers between devices: none -> 44.1 us  [on_device(): small_grads = lax.psum(one_axis, 'grp')]
    reduce_scatter x1, waiting for transfers between devices: 0.02 us -> 22.7 us  [on_device(): lax.psum_scatter(grad_proj.astype(jnp.bfloat16), 'grp', scatter_dimension...]
    psum x1, waiting for transfers between devices: 176 us -> 158 us  [on_device(): lax.psum(contract(grad_beforeb, w_expand, 1, 1).astype(jnp.bfloat16), 'tp')]
  transfers between devices with their start and end apart: 12 -> 13, of which waited for: 7 -> 12; matrix products, arithmetic and copies ran while one was open for 24% -> 17% of each run, Pallas kernels for 0% -> 0%
where the time goes in v1:
time: 1430 us; the launch traced here: 1420 us
  waiting for transfers between devices  953 us (67%)
  matrix products  236 us (17%)
  other arithmetic  159 us (11%)
  local copies, waits for them, and re-layouts  40.8 us (3%)
  between operations  14.9 us (1%)
    psum x1, waiting for transfers between devices, on_device(): lax.psum(contract(active, w_reduce, 1, 1).astype(jnp.bfloat16), 'tp')  260 us
    psum x1, waiting for transfers between devices, on_device(): lax.psum(contract(context_all, w_proj, 1, 1).astype(jnp.bfloat16), 'tp')  169 us
    psum x1, waiting for transfers between devices, on_device(): lax.psum(contract(grad_beforeb, w_expand, 1, 1).astype(jnp.bfloat16), 'tp')  158 us
    dot_general x8, matrix products, contract(): lax.dot_general(left, right, (((left_dim,), (right_dim,)), ((), ())), pre...  103 us
    psum x1, waiting for transfers between devices, on_device(): lax.psum((query_value_full, bias_out_grad, up_bias_full, down_bias_grad,...  55.9 us
    reduce_scatter x1, waiting for transfers between devices, on_device(): lax.psum_scatter(grad_reduce.astype(jnp.bfloat16), 'grp', scatter_dimensi...  54.2 us
    reduce_scatter x1, waiting for transfers between devices, on_device(): lax.psum_scatter(grad_expand.astype(jnp.bfloat16), 'grp', scatter_dimensi...  52.7 us
    reduce_scatter x1, waiting for transfers between devices, on_device(): lax.psum_scatter(grad_attn.astype(jnp.bfloat16), 'grp', scatter_dimension...  44.5 us
  transfers between devices with their start and end apart: 13, of which 12 were waited for; matrix products, arithmetic and copies ran while one was open for 17% of the time, Pallas kernels for 0%

profile of v1, /device:TPU:8, one launch (start us, length us, event | category | flops | bytes accessed | tf_op | source)
XLA Modules:
  0.0 1418.4 jit_solution(1209002106334912166)
XLA Ops:
  21.6 34.0 %all-gather.5.cloned.1.call-done = bf16[2048,768]{1,0:T(8,128)(2,1)} async-done(((bf16[512,768]{1,0:T(8,128)(2,1)}), bf16[2048,768]{1,0:T(8,128)(2,1)}) %all-gather.5.cloned.1.call-update) | async-done | bytes 3145744 | tf_op jit(solution)/shard_map/all_gather | solution.py:54
  71.4 46.1 %while.28 = (s32[]{:T(128)}, bf16[4,512,2,128]{3,2,1,0:T(2,128)(2,1)}, f32[4,2,512]{2,1,0:T(2,128)}, s32[4]{0:T(128)S(1)}, s32[2048]{0:T(1024)S(1)}, /*index=5*/...) while((s32[]{:T(128)}, ...), condition=%wide.region_7.8_spmd.clone, body=%wide.region_4.7_spmd.clone.sunk | while | flops 1102183936 | bytes 32557260 | solution.py:129
  132.2 169.3 %all-reduce.9.cloned.1.call-done = bf16[2048,2048]{1,0:T(8,128)(2,1)} async-done(((bf16[2048,2048]{1,0:T(8,128)(2,1)}), bf16[2048,2048]{1,0:T(8,128)(2,1)}) %all-reduce.9.cloned.1.call-update) | async-done | bytes 8388624 | tf_op jit(solution)/shard_map/psum | solution.py:131
  301.5 17.6 %fusion.88 = (f32[2048]{0:T(1024)S(1)}, f32[2048,2048]{1,0:T(8,128)}, f32[2048,2048]{1,0:T(8,128)}) fusion(f32[2048]{0:T(1024)S(1)} %copy-done.28, bf16[2048,2048]{1,0:T(8,128)(2,1)} %all-reduce.9.cloned.1.call-done, bf16[2048,2048]{1,0:T(8,128)(2,1)} %param.20, f32[2048]{0:T(1024)S(1)} %add_rsqrt_fusion.1, f32[2048]{0:T(1024)S(1)} %broadcast_multiply_fusion.3), kind=kLoop, calls=%fused_computation.141 | loop fusion | flops 29358080 | bytes 50364416 | tf_op jit(solution)/shard_map/reduce_sum | solution.py:10
  326.7 11.8 subtract_multiply_fusion
  338.5 18.2 %all-gather.9.cloned.1.call-done = bf16[2048,1024]{1,0:T(8,128)(2,1)} async-done(((bf16[512,1024]{1,0:T(8,128)(2,1)}), bf16[2048,1024]{1,0:T(8,128)(2,1)}) %all-gather.9.cloned.1.call-update) | async-done | bytes 4194320 | tf_op jit(solution)/shard_map/all_gather | solution.py:56
  356.7 15.5 %fusion.75 = f32[2048,1024]{1,0:T(8,128)} fusion(bf16[2048,1024]{1,0:T(8,128)(2,1)} %all-gather.9.cloned.1.call-done, f32[2048,2048]{1,0:T(8,128)} %subtract_multiply_fusion, f32[2048]{0:T(1024)S(1)} %copy-done.33, f32[2048]{0:T(1024)S(1)} %copy-done.23), kind=kOutput, calls=%fused_computation.102 | convolution fusion | flops 8602517504 | bytes 29376512 | tf_op jit(solution)/shard_map/dot_general | solution.py:140
  372.2 39.5 %all-gather.11.cloned.1.call-done = bf16[2048,1024]{1,0:T(8,128)(2,1)} async-done(((bf16[512,1024]{1,0:T(8,128)(2,1)}), bf16[2048,1024]{1,0:T(8,128)(2,1)}) %all-gather.11.cloned.1.call-update) | async-done | bytes 4194320 | tf_op jit(solution)/shard_map/all_gather | solution.py:57
  411.7 19.5 %convert_reduce_fusion.1 = (f32[1024]{0:T(1024)}, bf16[2048,1024]{1,0:T(8,128)(2,1)S(1)}) fusion(f32[2048,1024]{1,0:T(8,128)} %fusion.75, f32[1024]{0:T(1024)S(1)} %dynamic_slice.59, bf16[2048,1024]{1,0:T(8,128)(2,1)} %all-gather.11.cloned.1.call-done, f32[2048]{0:T(1024)S(1)} %compare_convert_fusion, bf16[2048,2048]{1,0:T(8,128)(2,1)} %param.21), kind=kOutput, calls=%fused_computation.74 | convolution fusion | flops 8650750976 | bytes 25182208 | tf_op jit(solution)/shard_map/dot_general | solution.py:156
  444.1 18.0 %convolution_convert_fusion.2 = bf16[2048,2048]{1,0:T(8,128)(2,1)} fusion(bf16[2048,1024]{1,0:T(8,128)(2,1)} %all-gather.11.cloned.1.call-done, f32[2048,1024]{1,0:T(8,128)} %fusion.75, f32[1024]{0:T(1024)S(1)} %dynamic_slice.59), kind=kOutput, calls=%fused_computation.78 | convolution fusion | flops 8615100416 | bytes 20975616 | tf_op jit(solution)/shard_map/dot_general | solution.py:26
  462.2 157.6 %all-reduce.11.cloned.1.call-done = bf16[2048,2048]{1,0:T(8,128)(2,1)} async-done(((bf16[2048,2048]{1,0:T(8,128)(2,1)}), bf16[2048,2048]{1,0:T(8,128)(2,1)}) %all-reduce.11.cloned.1.call-update) | async-done | bytes 8388624 | tf_op jit(solution)/shard_map/psum | solution.py:161
  630.4 21.3 %convert_multiply_fusion = (f32[2048,2048]{1,0:T(8,128)}, f32[2048,2048]{1,0:T(8,128)}) fusion(bf16[2048,2048]{1,0:T(8,128)(2,1)} %param.21, f32[2048]{0:T(1024)S(1)} %compare_convert_fusion, f32[2048]{0:T(1024)S(1)} %broadcast_multiply_fusion, f32[2048]{0:T(1024)S(1)} %broadcast_multiply_fusion.1, f32[2048]{0:T(1024)S(1)} %copy-done.23, ...), kind=kLoop, calls=%fused_computation.59 | loop fusion | flops 46137344 | bytes 67158016 | tf_op jit(solution)/shard_map/mul | solution.py:152
  661.0 89.7 %while.29 = (s32[]{:T(128)}, f32[2048,2,128]{0,2,1:T(8,128)S(1)}, f32[2048,2,128]{0,2,1:T(8,128)}, bf16[4,512,2,128]{3,1,0,2:T(8,128)(2,1)}, s32[4]{0:T(128)S(1)...) while((s32[]{:T(128)}, f32[2048,2,128]{0,2,1:T(8,128)S(1)}, ...), condition=%wide.region_17.18_spmd.clone, body=%wide.region_15.17_spmd.clone.sunk | while | flops 2721709568 | bytes 97040784 | solution.py:220
  759.8 11.6 convolution_convert_fusion
  782.7 16.9 %fusion.61 = bf16[2048,1024]{1,0:T(8,128)(2,1)} fusion(bf16[2048,2048]{1,0:T(8,128)(2,1)} %param.21, f32[2048]{0:T(1024)S(1)} %copy-done.20, f32[2048,1024]{1,0:T(8,128)} %fusion.75, f32[1024]{0:T(1024)S(1)} %copy-done.31), kind=kOutput, calls=%fused_computation.91 | convolution fusion | flops 8625586176 | bytes 20983808 | tf_op jit(solution)/shard_map/dot_general | solution.py:26
  799.8 15.7 %convolution_convert_fusion.4 = bf16[2048,1024]{1,0:T(8,128)(2,1)} fusion(bf16[2048,1024]{1,0:T(8,128)(2,1)} %copy-done.37, f32[2048,2048]{1,0:T(8,128)} %subtract_multiply_fusion, f32[2048]{0:T(1024)S(1)} %copy-done.34, f32[2048]{0:T(1024)S(1)} %copy-done.24), kind=kOutput, calls=%fused_computation.92 | convolution fusion | flops 8604614656 | bytes 25182208 | tf_op jit(solution)/shard_map/dot_general | solution.py:26
  815.7 11.9 convolution_convert_fusion.5
  845.3 259.9 %all-reduce.17.cloned.1.call-done = (bf16[2048,2048]{1,0:T(8,128)(2,1)}, bf16[2048,2048]{1,0:T(8,128)(2,1)}) async-done(((bf16[2048,2048]{1,0:T(8,128)(2,1)}, bf16[2048,2048]{1,0:T(8,128)(2,1)}), (bf16[2048,2048]{1,0:T(8,128)(2,1)}, bf16[2048,2048]{1,0:T(8,128)(2,1)})) %all-reduce.17.cloned.1.call-update) | async-done | bytes 16777232 | tf_op jit(solution)/shard_map/psum | solution.py:143
  1113.8 22.7 %reduce-scatter.7.cloned.1.call-done = bf16[512,256]{1,0:T(8,128)(2,1)} async-done(((bf16[2048,256]{1,0:T(8,128)(2,1)}), bf16[512,256]{1,0:T(8,128)(2,1)}) %reduce-scatter.7.cloned.1.call-update) | async-done | bytes 262160 | tf_op jit(solution)/shard_map/reduce_scatter | solution.py:264
  1138.4 54.2 %reduce-scatter.11.cloned.1.call-done = bf16[512,1024]{1,0:T(8,128)(2,1)} async-done(((bf16[2048,1024]{1,0:T(8,128)(2,1)}), bf16[512,1024]{1,0:T(8,128)(2,1)}) %reduce-scatter.11.cloned.1.call-update) | async-done | bytes 1048592 | tf_op jit(solution)/shard_map/reduce_scatter | solution.py:270
  1195.4 52.7 %reduce-scatter.9.cloned.1.call-done = bf16[512,1024]{1,0:T(8,128)(2,1)} async-done(((bf16[2048,1024]{1,0:T(8,128)(2,1)}), bf16[512,1024]{1,0:T(8,128)(2,1)}) %reduce-scatter.9.cloned.1.call-update) | async-done | bytes 1048592 | tf_op jit(solution)/shard_map/reduce_scatter | solution.py:267
  1250.9 44.5 %reduce-scatter.5.cloned.1.call-done = bf16[512,768]{1,0:T(8,128)(2,1)} async-done(((bf16[2048,768]{1,0:T(8,128)(2,1)}), bf16[512,768]{1,0:T(8,128)(2,1)}) %reduce-scatter.5.cloned.1.call-update) | async-done | bytes 786448 | tf_op jit(solution)/shard_map/reduce_scatter | solution.py:261
  1297.7 55.9 %all-reduce.13.cloned.1.call-done = (f32[4096]{0:T(1024)}, f32[2048]{0:T(1024)}, f32[8192]{0:T(1024)}, f32[2048]{0:T(1024)}, f32[2048]{0:T(1024)}, /*index=5*/f32[2048]{0:T(1024)}, f32[2048]{0:T(1024)}, f32[2048]{0:T(1024)}) async-done(((f32[4096]{0:T(1024)}, f32[2048]{0:T(1024)}, f32[8192]{0:T(1024)}, f32[2048]{0:T(1024)}, f32[2048]{0:T(1024)}, /*index=5*/f32[2048]{0:T(1024)}, f32[2048]{0:T(1024)}, ...) | async-done | bytes 98320 | tf_op jit(solution)/shard_map/psum | solution.py:274
  1356.8 44.1 %all-reduce.15.cloned.1.call-done = (f32[4096]{0:T(1024)}, f32[2048]{0:T(1024)}, f32[8192]{0:T(1024)}, f32[2048]{0:T(1024)}, f32[2048]{0:T(1024)}, /*index=5*/f32[2048]{0:T(1024)}, f32[2048]{0:T(1024)}, f32[2048]{0:T(1024)}) async-done(((f32[4096]{0:T(1024)}, f32[2048]{0:T(1024)}, f32[8192]{0:T(1024)}, f32[2048]{0:T(1024)}, f32[2048]{0:T(1024)}, /*index=5*/f32[2048]{0:T(1024)}, f32[2048]{0:T(1024)}, ...) | async-done | bytes 98320 | tf_op jit(solution)/shard_map/psum | solution.py:287
  (280 shorter events, 277.1 us)
Async XLA Ops:
  7.2 48.4 %all-gather.5.cloned.1.call-start = ((), (), s32[]{:S(2)}) async-start(), calls=%async_computation.4 | async-start | bytes 3932160 | tf_op jit(solution)/shard_map/all_gather | solution.py:54
  9.6 107.9 %all-gather.7.cloned.1.call-start = ((), (), s32[]{:S(2)}) async-start(), calls=%async_computation.5 | async-start | bytes 1310720 | tf_op jit(solution)/shard_map/all_gather | solution.py:55
  11.5 290.1 %all-reduce.9.cloned.1.call-start = ((), (), s32[]{:S(2)}) async-start(), calls=%async_computation.6 | async-start | bytes 16777216 | tf_op jit(solution)/shard_map/psum | solution.py:131
  13.4 42.2 %copy-start.25 = (f32[2048]{0:T(1024)S(1)}, f32[2048]{0:T(1024)}, u32[]{:S(2)}) copy-start(f32[2048]{0:T(1024)} %param.32) | copy-start | bytes 24580
  13.4 42.2 %copy-start.35 = (f32[2048]{0:T(1024)S(1)}, f32[2048]{0:T(1024)}, u32[]{:S(2)}) copy-start(f32[2048]{0:T(1024)} %param.33) | copy-start | bytes 24580
  19.2 282.3 %copy-start.16 = (f32[2048]{0:T(1024)}, f32[2048]{0:T(1024)S(1)}, u32[]{:S(2)}) copy-start(f32[2048]{0:T(1024)S(1)} %broadcast_multiply_fusion.3) | copy-start | bytes 24580
  21.6 280.0 %copy-start.21 = (f32[2048]{0:T(1024)}, f32[2048]{0:T(1024)S(1)}, u32[]{:S(2)}) copy-start(f32[2048]{0:T(1024)S(1)} %add_rsqrt_fusion.1) | copy-start | bytes 24580
  125.8 175.8 %copy-start.28 = (f32[2048]{0:T(1024)S(1)}, f32[2048]{0:T(1024)}, u32[]{:S(2)}) copy-start(f32[2048]{0:T(1024)} %param.27) | copy-start | bytes 24580
  125.8 230.8 %all-gather.9.cloned.1.call-start = ((), (), s32[]{:S(2)}) async-start(), calls=%async_computation.7 | async-start | bytes 5242880 | tf_op jit(solution)/shard_map/all_gather | solution.py:56
  128.6 283.0 %all-gather.11.cloned.1.call-start = ((), (), s32[]{:S(2)}) async-start(), calls=%async_computation.8 | async-start | bytes 5242880 | tf_op jit(solution)/shard_map/all_gather | solution.py:57
  131.4 488.3 %all-reduce.11.cloned.1.call-start = ((), (), s32[]{:S(2)}) async-start(), calls=%async_computation.9 | async-start | bytes 16777216 | tf_op jit(solution)/shard_map/psum | solution.py:161
  131.5 498.6 %copy-start.19 = (f32[2048]{0:T(1024)}, f32[2048]{0:T(1024)S(1)}, u32[]{:S(2)}) copy-start(f32[2048]{0:T(1024)S(1)} %compare_convert_fusion) | copy-start | bytes 24580
  132.2 311.9 %copy-start.30 = (f32[1024]{0:T(1024)}, f32[1024]{0:T(1024)S(1)}, u32[]{:S(2)}) copy-start(f32[1024]{0:T(1024)S(1)} %dynamic_slice.59) | copy-start | bytes 12292
  326.7 30.0 %copy-start.23 = (f32[2048]{0:T(1024)S(1)}, f32[2048]{0:T(1024)}, u32[]{:S(2)}) copy-start(f32[2048]{0:T(1024)} %param.34) | copy-start | bytes 24580
  326.7 30.0 %copy-start.33 = (f32[2048]{0:T(1024)S(1)}, f32[2048]{0:T(1024)}, u32[]{:S(2)}) copy-start(f32[2048]{0:T(1024)} %param.35) | copy-start | bytes 24580
  444.1 661.2 %all-reduce.17.cloned.1.call-start = ((), (), s32[]{:S(2)}) async-start(), calls=%async_computation.16 | async-start | bytes 33554432 | tf_op jit(solution)/shard_map/psum | solution.py:143
  771.4 365.1 %reduce-scatter.7.cloned.1.call-start = ((), (), s32[]{:S(2)}) async-start(), calls=%async_computation.11 | async-start | bytes 1310720 | tf_op jit(solution)/shard_map/reduce_scatter | solution.py:264
  782.6 409.9 %reduce-scatter.11.cloned.1.call-start = ((), (), s32[]{:S(2)}) async-start(), calls=%async_computation.13 | async-start | bytes 5242880 | tf_op jit(solution)/shard_map/reduce_scatter | solution.py:270
  799.7 448.4 %reduce-scatter.9.cloned.1.call-start = ((), (), s32[]{:S(2)}) async-start(), calls=%async_computation.12 | async-start | bytes 5242880 | tf_op jit(solution)/shard_map/reduce_scatter | solution.py:267
  815.6 479.8 %reduce-scatter.5.cloned.1.call-start = ((), (), s32[]{:S(2)}) async-start(), calls=%async_computation.10 | async-start | bytes 3932160 | tf_op jit(solution)/shard_map/reduce_scatter | solution.py:261
  827.5 526.1 %all-reduce.13.cloned.1.call-start = ((), (), s32[]{:S(2)}) async-start(), calls=%async_computation.14 | async-start | bytes 196608 | tf_op jit(solution)/shard_map/psum | solution.py:274
  845.3 268.4 %copy-start.18 = (f32[16,2,128]{2,1,0:T(2,128)}, f32[16,2,128]{2,1,0:T(2,128)S(1)}, u32[]{:S(2)}) copy-start(f32[16,2,128]{2,1,0:T(2,128)S(1)} %constant_dynamic-update-slice_fusion) | copy-start | bytes 49156
  1108.5 245.2 %copy-start.27 = (f32[2048]{0:T(1024)S(1)}, f32[2048]{0:T(1024)}, u32[]{:S(2)}) copy-start(f32[2048]{0:T(1024)} %param.31) | copy-start | bytes 24580
  1113.7 287.2 %all-reduce.15.cloned.1.call-start = ((), (), s32[]{:S(2)}) async-start(), calls=%async_computation.15 | async-start | bytes 196608 | tf_op jit(solution)/shard_map/psum | solution.py:287
  (39 other events, 330.5 us)
Sparse Core Ops, SparseCore 0:
  10.4 45.1 all-gather.4
  58.0 26.6 all-gather.6
  125.9 175.5 all-reduce.8
  303.8 52.8 all-gather.8
  358.9 52.6 all-gather.10
  444.2 175.5 all-reduce.10
  771.5 333.6 all-reduce.16
  1108.7 27.8 reduce-scatter.6
  1139.8 52.6 reduce-scatter.10
  1195.4 52.6 reduce-scatter.8
  1251.4 43.9 reduce-scatter.4
  1299.5 54.0 all-reduce.12
  1357.1 43.7 all-reduce.14
